TPU v7x, 32 devices: a whole 2x2x4 slice. The times are simulated.
32 devices in a mesh: sx: 8 (over y, x, core), sy: 4 (over z).
Axes of the slice: x: 2, y: 2, z: 4, core: 2. Of those that a mesh axis runs over, the one named last changes fastest.
Arguments:
- schur_x: float32 [16, 4, 512, 512], P('sx', 'sy'), may hold values from -1 to 5, as said below
- schur_y: float32 [8, 8, 512, 512], P('sx', 'sy'), may hold values from -1 to 5, as said below
- residual_x: float32 [16, 4, 32, 512], P('sx', 'sy'), may hold values from -36 to 36
- residual_y: float32 [8, 8, 32, 512], P('sx', 'sy'), may hold values from -36 to 36
- basis_x: float32 [16, 4, 6, 512], P('sx', 'sy'), may hold values from -0.9 to 0.9
- basis_y: float32 [8, 8, 6, 512], P('sx', 'sy'), may hold values from -0.9 to 0.9
- couple_x: float32 [8, 4, 6, 6], P('sx', 'sy'), may hold values from -0.3 to 0.1
- couple_y: float32 [8, 4, 6, 6], P('sx', 'sy'), may hold values from -0.3 to 0.1
- coarse_shift: float32 [8, 4, 6], P('sx', 'sy'), may hold values from 0.05 to 0.5
Outputs:
- average_x: float32 [16, 4, 32, 512], P('sx', 'sy')
- average_y: float32 [8, 8, 32, 512], P('sx', 'sy')
- coarse_values: float32 [8, 4, 6, 32], P('sx', 'sy')
Inputs may be any that keep to these rules, and one draw needn't show every extreme that they name: `schur_x`: every block is symmetric positive definite. `schur_y`: every block is symmetric positive definite.
All inputs are finite; a program needn't handle non-finite values.
Results may differ from a plain program's by a relative error of at most 0.0003.
Values sent between devices are 32-bit elements; how exact they have to be, the bound alone decides.
No kernel may reach another device: no remote copies, remote signals or barrier semaphores. Data moves between devices by JAX's collectives and lax.ppermute only.
A program may use at most 128 MiB of HBM per device.

v0:
```python
import jax
import jax.numpy as jnp
from jax import lax
from jax.sharding import PartitionSpec as P

CITERS = 8
HIGH = lax.Precision.HIGHEST


def shifted(array, axis, by):
    count = lax.axis_size(axis)
    pairs = [(i, i + by) for i in range(count) if 0 <= i + by < count]
    return lax.ppermute(array, axis, pairs)


def with_halo(cells, sides, width):
    for axis, dim in sides:
        count = lax.axis_size(axis)
        ends = count - 1
        head = lax.slice_in_dim(cells, 0, width, axis=dim)
        tail = lax.slice_in_dim(cells, cells.shape[dim] - width, cells.shape[dim], axis=dim)
        cells = jnp.concatenate(
            [
                lax.ppermute(tail, axis, [(i, (i + 1) % count) for i in range(ends)]),
                cells,
                lax.ppermute(head, axis, [((i + 1) % count, i) for i in range(ends)]),
            ],
            axis=dim,
        )
    return cells


def face_average(s_low, s_high, r_low, r_high):
    summed = s_low + s_high
    factor = jnp.linalg.cholesky(summed)
    right_side = jnp.dot(s_low, r_low.T, precision=HIGH) + jnp.dot(s_high, r_high.T, precision=HIGH)
    forward = jax.scipy.linalg.solve_triangular(factor, right_side, lower=True)
    solved = jax.scipy.linalg.solve_triangular(factor, forward, lower=True, trans=1)
    return solved.T


def shards(
    schur_x, schur_y, residual_x, residual_y, basis_x, basis_y, couple_x, couple_y, coarse_shift
):
    row_index = lax.axis_index("sx")
    row_count = lax.axis_size("sx")
    col_index = lax.axis_index("sy")
    col_count = lax.axis_size("sy")
    link_x = couple_x[0, 0] * (row_index > 0).astype(jnp.float32)
    link_y = couple_y[0, 0] * (col_index > 0).astype(jnp.float32)
    above_x = shifted((schur_x[0, 0], residual_x[0, 0], link_x), "sx", -1)
    above_y = shifted((schur_y[0, 0], residual_y[0, 0], link_y), "sy", -1)
    upper_x = face_average(schur_x[1, 0], above_x[0], residual_x[1, 0], above_x[1])
    upper_y = face_average(schur_y[0, 1], above_y[0], residual_y[0, 1], above_y[1])
    upper_x = jnp.where(row_index == row_count - 1, residual_x[1, 0], upper_x)
    upper_y = jnp.where(col_index == col_count - 1, residual_y[0, 1], upper_y)
    lower_x = shifted(upper_x, "sx", 1)
    lower_y = shifted(upper_y, "sy", 1)
    next_x = above_x[2]
    next_y = above_y[2]
    lower_x = jnp.where(row_index == 0, residual_x[0, 0], lower_x)
    upper_x = jnp.where(row_index == row_count - 1, residual_x[1, 0], upper_x)
    lower_y = jnp.where(col_index == 0, residual_y[0, 0], lower_y)
    upper_y = jnp.where(col_index == col_count - 1, residual_y[0, 1], upper_y)
    rhs_coarse = jnp.einsum("spf,srf->pr", basis_x[:, 0], residual_x[:, 0], precision=HIGH)
    rhs_coarse = rhs_coarse + jnp.einsum("spf,srf->pr", basis_y[0], residual_y[0], precision=HIGH)
    diagonal = (
        jnp.sum(jnp.abs(link_x), axis=0)
        + jnp.sum(jnp.abs(next_x), axis=1)
        + jnp.sum(jnp.abs(link_y), axis=0)
        + jnp.sum(jnp.abs(next_y), axis=1)
        + coarse_shift[0, 0]
    )
    coarse = jnp.zeros_like(rhs_coarse)
    remain = rhs_coarse

    def squares(values):
        return lax.psum(jnp.sum(values * values, axis=0), ("sx", "sy"))

    direction = rhs_coarse
    norm_now = squares(remain)
    for sweep_index in range(CITERS):
        padded = with_halo(direction[None, None], (("sx", 0), ("sy", 1)), 1)
        image = diagonal[:, None] * direction
        image = image + jnp.dot(link_x.T, padded[0, 1], precision=HIGH)
        image = image + jnp.dot(next_x, padded[2, 1], precision=HIGH)
        image = image + jnp.dot(link_y.T, padded[1, 0], precision=HIGH)
        image = image + jnp.dot(next_y, padded[1, 2], precision=HIGH)
        curve = lax.psum(jnp.sum(direction * image, axis=0), ("sx", "sy"))
        alpha = norm_now / curve
        coarse = coarse + alpha * direction
        remain = remain - alpha * image
        norm_next = squares(remain)
        direction = remain + norm_next / norm_now * direction
        norm_now = norm_next
    lift_x = jnp.einsum("pr,spf->srf", coarse, basis_x[:, 0], precision=HIGH)
    lift_y = jnp.einsum("pr,spf->srf", coarse, basis_y[0], precision=HIGH)
    out_x = (jnp.stack([lower_x, upper_x], axis=0) + lift_x)[:, None]
    out_y = (jnp.stack([lower_y, upper_y], axis=0) + lift_y)[None]
    return (out_x, out_y, coarse[None, None])


def solution(mesh):
    placed = (
        P("sx", "sy", None, None),
        P("sx", "sy", None, None),
        P("sx", "sy", None, None),
        P("sx", "sy", None, None),
        P("sx", "sy", None, None),
        P("sx", "sy", None, None),
        P("sx", "sy", None, None),
        P("sx", "sy", None, None),
        P("sx", "sy", None),
    )
    return jax.shard_map(
        shards,
        mesh=mesh,
        in_specs=placed,
        out_specs=(P("sx", "sy", None, None), P("sx", "sy", None, None), P("sx", "sy", None, None)),
        check_vma=False,
    )
```

profile of v0, /device:TPU:1, one launch (start us, length us, event | category | flops | bytes accessed | tf_op | source)
XLA Modules:
  0.0 1094.7 jit_solution(9684428249556823600)
XLA Ops:
  27.0 40.4 %all-reduce.1 = (f32[32]{0:T(128)S(1)}, f32[32]{0:T(128)S(1)}) all-reduce(f32[32]{0:T(128)S(1)} %get-tuple-element.45, f32[32]{0:T(128)S(1)} %get-tuple-element.44), channel_id=1, replica_groups=mesh['sx'=8,'sy'=4] {'sx','sy'}, use_global_device_ids=true, to_apply=%region_9.13 | all-reduce | flops 64 | bytes 512 | tf_op jit(solution)/shard_map/psum | solution.py:78
  67.5 41.3 %psum.114 = f32[32]{0:T(128)S(1)} all-reduce(f32[32]{0:T(128)S(1)} %multiply_reduce_fusion.12), channel_id=1, replica_groups=mesh['sx'=8,'sy'=4] {'sx','sy'}, use_global_device_ids=true, to_apply=%region_17.21 | all-reduce | flops 32 | bytes 256 | tf_op jit(solution)/shard_map/psum | solution.py:78
  127.3 39.4 %psum.115 = f32[32]{0:T(128)S(1)} all-reduce(f32[32]{0:T(128)S(1)} %get-tuple-element.109), channel_id=1, replica_groups=mesh['sx'=8,'sy'=4] {'sx','sy'}, use_global_device_ids=true, to_apply=%region_19.23 | all-reduce | flops 32 | bytes 256 | tf_op jit(solution)/shard_map/psum | solution.py:89
  166.7 40.3 %psum.116 = f32[32]{0:T(128)S(1)} all-reduce(f32[32]{0:T(128)S(1)} %get-tuple-element.74), channel_id=1, replica_groups=mesh['sx'=8,'sy'=4] {'sx','sy'}, use_global_device_ids=true, to_apply=%region_21.25 | all-reduce | flops 32 | bytes 256 | tf_op jit(solution)/shard_map/psum | solution.py:78
  225.6 40.9 %psum.117 = f32[32]{0:T(128)S(1)} all-reduce(f32[32]{0:T(128)S(1)} %get-tuple-element.111), channel_id=1, replica_groups=mesh['sx'=8,'sy'=4] {'sx','sy'}, use_global_device_ids=true, to_apply=%region_23.27 | all-reduce | flops 32 | bytes 256 | tf_op jit(solution)/shard_map/psum | solution.py:89
  266.5 41.2 %psum.118 = f32[32]{0:T(128)S(1)} all-reduce(f32[32]{0:T(128)S(1)} %get-tuple-element.72), channel_id=1, replica_groups=mesh['sx'=8,'sy'=4] {'sx','sy'}, use_global_device_ids=true, to_apply=%region_25.29 | all-reduce | flops 32 | bytes 256 | tf_op jit(solution)/shard_map/psum | solution.py:78
  327.5 41.1 %psum.119 = f32[32]{0:T(128)S(1)} all-reduce(f32[32]{0:T(128)S(1)} %get-tuple-element.113), channel_id=1, replica_groups=mesh['sx'=8,'sy'=4] {'sx','sy'}, use_global_device_ids=true, to_apply=%region_27.31 | all-reduce | flops 32 | bytes 256 | tf_op jit(solution)/shard_map/psum | solution.py:89
  368.6 40.1 %psum.120 = f32[32]{0:T(128)S(1)} all-reduce(f32[32]{0:T(128)S(1)} %get-tuple-element.70), channel_id=1, replica_groups=mesh['sx'=8,'sy'=4] {'sx','sy'}, use_global_device_ids=true, to_apply=%region_29.33 | all-reduce | flops 32 | bytes 256 | tf_op jit(solution)/shard_map/psum | solution.py:78
  425.7 39.1 %psum.121 = f32[32]{0:T(128)S(1)} all-reduce(f32[32]{0:T(128)S(1)} %get-tuple-element.115), channel_id=1, replica_groups=mesh['sx'=8,'sy'=4] {'sx','sy'}, use_global_device_ids=true, to_apply=%region_31.35 | all-reduce | flops 32 | bytes 256 | tf_op jit(solution)/shard_map/psum | solution.py:89
  464.8 40.4 %psum.122 = f32[32]{0:T(128)S(1)} all-reduce(f32[32]{0:T(128)S(1)} %get-tuple-element.68), channel_id=1, replica_groups=mesh['sx'=8,'sy'=4] {'sx','sy'}, use_global_device_ids=true, to_apply=%region_33.37 | all-reduce | flops 32 | bytes 256 | tf_op jit(solution)/shard_map/psum | solution.py:78
  520.9 52.7 %psum.123 = f32[32]{0:T(128)S(1)} all-reduce(f32[32]{0:T(128)S(1)} %get-tuple-element.117), channel_id=1, replica_groups=mesh['sx'=8,'sy'=4] {'sx','sy'}, use_global_device_ids=true, to_apply=%region_35.39 | all-reduce | flops 32 | bytes 256 | tf_op jit(solution)/shard_map/psum | solution.py:89
  573.6 41.2 %psum.124 = f32[32]{0:T(128)S(1)} all-reduce(f32[32]{0:T(128)S(1)} %get-tuple-element.66), channel_id=1, replica_groups=mesh['sx'=8,'sy'=4] {'sx','sy'}, use_global_device_ids=true, to_apply=%region_37.41 | all-reduce | flops 32 | bytes 256 | tf_op jit(solution)/shard_map/psum | solution.py:78
  631.6 39.8 %psum.125 = f32[32]{0:T(128)S(1)} all-reduce(f32[32]{0:T(128)S(1)} %get-tuple-element.119), channel_id=1, replica_groups=mesh['sx'=8,'sy'=4] {'sx','sy'}, use_global_device_ids=true, to_apply=%region_39.43 | all-reduce | flops 32 | bytes 256 | tf_op jit(solution)/shard_map/psum | solution.py:89
  671.9 40.3 %psum.126 = f32[32]{0:T(128)S(1)} all-reduce(f32[32]{0:T(128)S(1)} %multiply_reduce_fusion), channel_id=1, replica_groups=mesh['sx'=8,'sy'=4] {'sx','sy'}, use_global_device_ids=true, to_apply=%region_41.45 | all-reduce | flops 32 | bytes 256 | tf_op jit(solution)/shard_map/psum | solution.py:78
  726.0 23.5 %collective-permute-done.36 = f32[3,1,6,32]{3,2,1,0:T(8,128)S(1)} collective-permute-done((f32[3,1,6,32]{3,2,1,0:T(8,128)S(1)}, f32[3,1,6,32]{3,2,1,0:T(8,128)S(1)}, u32[]{:S(2)}, u32[]{:S(2)}) %collective-permute-start.36) | collective-permute-done | bytes 2336 | tf_op jit(solution)/shard_map/ppermute | solution.py:26
  755.8 39.7 %psum.127 = f32[32]{0:T(128)S(1)} all-reduce(f32[32]{0:T(128)S(1)} %fusion.26), channel_id=1, replica_groups=mesh['sx'=8,'sy'=4] {'sx','sy'}, use_global_device_ids=true, to_apply=%region_43.47 | all-reduce | flops 32 | bytes 256 | tf_op jit(solution)/shard_map/psum | solution.py:89
  799.2 11.7 %cholesky.286 = f32[128,128]{1,0:T(8,128)S(1)} custom-call(f32[128,128]{1,0:T(8,128)S(1)} %cholesky.426), custom_call_target="Cholesky" | custom-call | tf_op jit(solution)/shard_map/jit(cholesky)/cholesky | solution.py:35
  810.9 9.8 custom-call.31
  823.4 11.7 %cholesky.305 = f32[128,128]{1,0:T(8,128)S(1)} custom-call(f32[128,128]{1,0:T(8,128)S(1)} %cholesky.430), custom_call_target="Cholesky" | custom-call | tf_op jit(solution)/shard_map/jit(cholesky)/cholesky | solution.py:35
  835.2 10.2 custom-call.32
  846.9 11.7 %cholesky.326 = f32[128,128]{1,0:T(8,128)S(1)} custom-call(f32[128,128]{1,0:T(8,128)S(1)} %cholesky.435), custom_call_target="Cholesky" | custom-call | tf_op jit(solution)/shard_map/jit(cholesky)/cholesky | solution.py:35
  859.4 9.8 custom-call.33
  870.6 11.9 %cholesky.343 = f32[128,128]{1,0:T(8,128)S(1)} custom-call(f32[128,128]{1,0:T(8,128)S(1)} %slice_subtract_fusion.5), custom_call_target="Cholesky" | custom-call | tf_op jit(solution)/shard_map/jit(cholesky)/cholesky | solution.py:35
  887.3 10.3 while.8
  897.5 40.7 %custom-call.35 = f32[4,128,128]{1,2,0:T(8,128)} custom-call(f32[4,128,128]{2,1,0:T(8,128)} %get-tuple-element.35), custom_call_target="InvertDiagBlocksLowerTriangular" | custom-call | tf_op jit(solution)/shard_map/jit(_solve_triangular)/triangular_solve | solution.py:38
  953.5 11.7 %cholesky.358 = f32[128,128]{1,0:T(8,128)S(1)} custom-call(f32[128,128]{1,0:T(8,128)S(1)} %cholesky.439), custom_call_target="Cholesky" | custom-call | tf_op jit(solution)/shard_map/jit(cholesky)/cholesky | solution.py:35
  965.2 9.8 custom-call.36
  975.8 11.7 %cholesky.377 = f32[128,128]{1,0:T(8,128)S(1)} custom-call(f32[128,128]{1,0:T(8,128)S(1)} %cholesky.443), custom_call_target="Cholesky" | custom-call | tf_op jit(solution)/shard_map/jit(cholesky)/cholesky | solution.py:35
  987.6 10.0 custom-call.37
  998.3 11.7 %cholesky.398 = f32[128,128]{1,0:T(8,128)S(1)} custom-call(f32[128,128]{1,0:T(8,128)S(1)} %cholesky.448), custom_call_target="Cholesky" | custom-call | tf_op jit(solution)/shard_map/jit(cholesky)/cholesky | solution.py:35
  1021.1 11.7 %cholesky.415 = f32[128,128]{1,0:T(8,128)S(1)} custom-call(f32[128,128]{1,0:T(8,128)S(1)} %slice_subtract_fusion.4), custom_call_target="Cholesky" | custom-call | tf_op jit(solution)/shard_map/jit(cholesky)/cholesky | solution.py:35
  1045.4 39.3 %custom-call.40 = f32[4,128,128]{1,2,0:T(8,128)S(1)} custom-call(f32[4,128,128]{2,1,0:T(8,128)S(1)} %get-tuple-element.37), custom_call_target="InvertDiagBlocksLowerTriangular" | custom-call | tf_op jit(solution)/shard_map/jit(_solve_triangular)/triangular_solve | solution.py:38
  (319 shorter events, 230.4 us)
Async XLA Ops:
  3.7 14.8 %collective-permute-start.6 = (f32[1,1,6,32]{3,2,1,0:T(8,128)S(1)}, f32[1,1,6,32]{3,2,1,0:T(8,128)S(1)}, u32[]{:S(2)}, u32[]{:S(2)}) collective-permute-start(f32[1,1,6,32]{3,2,1,0:T(8,128)S(1)} %bitcast.395), channel_id=1, source_target_pairs={{4,0},{8,4},{12,8},{16,12},{20,16},{24,20},{28,24},{5,1},{9,5},{13... | collective-permute-start | bytes 2312 | tf_op jit(solution)/shard_map/ppermute | solution.py:26
  5.6 12.9 %collective-permute-start.5 = (f32[1,1,6,32]{3,2,1,0:T(8,128)S(1)}, f32[1,1,6,32]{3,2,1,0:T(8,128)S(1)}, u32[]{:S(2)}, u32[]{:S(2)}) collective-permute-start(f32[1,1,6,32]{3,2,1,0:T(8,128)S(1)} %bitcast.396), channel_id=1, source_target_pairs={{0,4},{4,8},{8,12},{12,16},{16,20},{20,24},{24,28},{1,5},{5,9},{9,... | collective-permute-start | bytes 2312 | tf_op jit(solution)/shard_map/ppermute | solution.py:24
  12.8 4.9 collective-permute-start.3
  18.5 6.1 collective-permute-start.8
  19.8 5.4 collective-permute-start.7
  108.8 10.0 collective-permute-start.10
  112.2 6.6 collective-permute-start.9
  117.5 967.2 %collective-permute-start.38 = (f32[32,512]{1,0:T(8,128)}, f32[32,512]{1,0:T(8,128)}, u32[]{:S(2)}, u32[]{:S(2)}) collective-permute-start(f32[32,512]{1,0:T(8,128)} %slice_bitcast_fusion.8), channel_id=1, source_target_pairs={{1,0},{2,1},{3,2},{5,4},{6,5},{7,6},{9,8},{10,9},{11,10},{13,12},{... | collective-permute-start | bytes 196616 | tf_op jit(solution)/shard_map/ppermute | solution.py:13
  118.8 6.1 collective-permute-start.12
  120.1 5.4 collective-permute-start.11
  207.1 10.6 collective-permute-start.14
  210.4 7.2 collective-permute-start.13
  215.7 722.5 %collective-permute-start.1 = (f32[32,512]{1,0:T(8,128)}, f32[32,512]{1,0:T(8,128)}, u32[]{:S(2)}, u32[]{:S(2)}) collective-permute-start(f32[32,512]{1,0:T(8,128)} %slice_bitcast_fusion.9), channel_id=1, source_target_pairs={{4,0},{8,4},{12,8},{16,12},{20,16},{24,20},{28,24},{5,1},{9,5},{13... | collective-permute-start | bytes 196616 | tf_op jit(solution)/shard_map/ppermute | solution.py:13
  217.7 5.4 collective-permute-start.16
  307.7 13.2 %collective-permute-start.18 = (f32[1,1,6,32]{3,2,1,0:T(8,128)S(1)}, f32[1,1,6,32]{3,2,1,0:T(8,128)S(1)}, u32[]{:S(2)}, u32[]{:S(2)}) collective-permute-start(f32[1,1,6,32]{3,2,1,0:T(8,128)S(1)} %bitcast.402), channel_id=1, source_target_pairs={{4,0},{8,4},{12,8},{16,12},{20,16},{24,20},{28,24},{5,1},{9,5},{13... | collective-permute-start | bytes 2312 | tf_op jit(solution)/shard_map/ppermute | solution.py:26
  311.1 9.8 collective-permute-start.17
  319.0 478.4 %collective-permute-start = (f32[512,512]{0,1:T(8,128)}, f32[512,512]{0,1:T(8,128)S(1)}, u32[]{:S(2)}, u32[]{:S(2)}) collective-permute-start(f32[512,512]{0,1:T(8,128)} %bitcast.3), channel_id=1, source_target_pairs={{4,0},{8,4},{12,8},{16,12},{20,16},{24,20},{28,24},{5,1},{9,5},{13... | collective-permute-start | bytes 3145736 | tf_op jit(solution)/shard_map/ppermute | solution.py:13
  320.9 5.4 collective-permute-start.20
  408.8 10.4 collective-permute-start.22
  412.3 6.9 collective-permute-start.21
  419.2 5.4 collective-permute-start.24
  505.3 8.9 collective-permute-start.26
  508.7 5.5 collective-permute-start.25
  514.2 5.6 collective-permute-start.28
  614.9 9.5 collective-permute-start.30
  618.3 6.1 collective-permute-start.29
  624.4 5.4 collective-permute-start.32
  712.3 10.3 collective-permute-start.34
  715.7 8.2 collective-permute-start.33
  722.6 228.8 %collective-permute-start.37 = (f32[512,512]{0,1:T(8,128)}, f32[512,512]{0,1:T(8,128)}, u32[]{:S(2)}, u32[]{:S(2)}) collective-permute-start(f32[512,512]{0,1:T(8,128)} %bitcast.390), channel_id=1, source_target_pairs={{1,0},{2,1},{3,2},{5,4},{6,5},{7,6},{9,8},{10,9},{11,10},{13,12},{... | collective-permute-start | bytes 3145736 | tf_op jit(solution)/shard_map/ppermute | solution.py:13
  724.6 24.9 %collective-permute-start.36 = (f32[3,1,6,32]{3,2,1,0:T(8,128)S(1)}, f32[3,1,6,32]{3,2,1,0:T(8,128)S(1)}, u32[]{:S(2)}, u32[]{:S(2)}) collective-permute-start(f32[3,1,6,32]{3,2,1,0:T(8,128)S(1)} %pad_maximum_fusion.7), channel_id=1, source_target_pairs={{1,0},{2,1},{3,2},{5,4},{6,5},{7,6},{9,8},{10,9},{11,10},{13,12},{... | collective-permute-start | bytes 6920 | tf_op jit(solution)/shard_map/ppermute | solution.py:26
  946.1 145.2 %collective-permute-start.2 = (f32[32,512]{1,0:T(8,128)}, f32[32,512]{1,0:T(8,128)}, u32[]{:S(2)}, u32[]{:S(2)}) collective-permute-start(f32[32,512]{1,0:T(8,128)} %get-tuple-element.77), channel_id=1, source_target_pairs={{0,4},{4,8},{8,12},{12,16},{16,20},{20,24},{24,28},{1,5},{5,9},{9,... | collective-permute-start | bytes 196616 | tf_op jit(solution)/shard_map/ppermute | solution.py:13
  (29 other events, 1720.2 us)
where the time goes:
time: 1110 us; the launch traced here: 1090 us
  blocking collectives  618 us (56%)
  other arithmetic  248 us (22%)
  starting transfers between devices  116 us (10%)
  matrix products  38.3 us (3%)
  local copies, waits for them, and re-layouts  36.8 us (3%)
  waiting for transfers between devices  30.2 us (3%)
    psum x8, blocking collectives, squares(): return lax.psum(jnp.sum(values * values, axis=0), ('sx', 'sy'))  325 us
    psum x7, blocking collectives, shards(): curve = lax.psum(jnp.sum(direction * image, axis=0), ('sx', 'sy'))  293 us
    another operation x28, other arithmetic, face_average(): factor = jnp.linalg.cholesky(summed)  158 us
    another operation x5, other arithmetic, face_average(): jax.scipy.linalg.solve_triangular(factor, forward, lower=True, trans=1)  80.8 us
    ppermute x16, starting transfers between devices, with_halo(): lax.ppermute(tail, axis, [(i, (i + 1) % count) for i in range(ends)])  63.3 us
    ppermute x16, starting transfers between devices, with_halo(): lax.ppermute(head, axis, [((i + 1) % count, i) for i in range(ends)])  36.3 us
    ppermute x16, waiting for transfers between devices, with_halo(): lax.ppermute(head, axis, [((i + 1) % count, i) for i in range(ends)])  23.5 us
  transfers between devices with their start and end apart: 40, of which 10 were waited for; matrix products, arithmetic and copies ran while one was open for 29% of the time, Pallas kernels for 0%

commit v1 on v0

--- a/solution.py
+++ b/solution.py
@@ -86,7 +86,7 @@
         image = image + jnp.dot(next_x, padded[2, 1], precision=HIGH)
         image = image + jnp.dot(link_y.T, padded[1, 0], precision=HIGH)
         image = image + jnp.dot(next_y, padded[1, 2], precision=HIGH)
-        curve = lax.psum(jnp.sum(direction * image, axis=0), ("sx", "sy"))
+        curve = lax.psum(lax.psum(jnp.sum(direction * image, axis=0), "sy"), "sx")
         alpha = norm_now / curve
         coarse = coarse + alpha * direction
         remain = remain - alpha * image

time: 1110 us -> 988 us (0.89)
  blocking collectives: 618 us -> 499 us
    psum x7 -> x16, blocking collectives: 293 us -> 195 us  [shards(): curve = lax.psum(lax.psum(jnp.sum(direction * image, axis=0), 'sy'), 'sx')]
    psum x8, blocking collectives: 325 us -> 304 us  [squares(): return lax.psum(jnp.sum(values * values, axis=0), ('sx', 'sy'))]
  transfers between devices with their start and end apart: 40 -> 40, of which waited for: 10 -> 10; matrix products, arithmetic and copies ran while one was open for 29% -> 32% of each run, Pallas kernels for 0% -> 0%
where the time goes in v1:
time: 988 us; the launch traced here: 975 us
  blocking collectives  499 us (51%)
  other arithmetic  248 us (25%)
  starting transfers between devices  116 us (12%)
  matrix products  37.6 us (4%)
  local copies, waits for them, and re-layouts  36.8 us (4%)
  waiting for transfers between devices  29.2 us (3%)
    psum x8, blocking collectives, squares(): return lax.psum(jnp.sum(values * values, axis=0), ('sx', 'sy'))  304 us
    psum x16, blocking collectives, shards(): curve = lax.psum(lax.psum(jnp.sum(direction * image, axis=0), 'sy'), 'sx')  195 us
    another operation x28, other arithmetic, face_average(): factor = jnp.linalg.cholesky(summed)  158 us
    another operation x5, other arithmetic, face_average(): jax.scipy.linalg.solve_triangular(factor, forward, lower=True, trans=1)  80.8 us
    ppermute x16, starting transfers between devices, with_halo(): lax.ppermute(tail, axis, [(i, (i + 1) % count) for i in range(ends)])  67.3 us
    ppermute x16, starting transfers between devices, with_halo(): lax.ppermute(head, axis, [((i + 1) % count, i) for i in range(ends)])  36.1 us
    ppermute x16, waiting for transfers between devices, with_halo(): lax.ppermute(head, axis, [((i + 1) % count, i) for i in range(ends)])  23.9 us
  transfers between devices with their start and end apart: 40, of which 10 were waited for; matrix products, arithmetic and copies ran while one was open for 32% of the time, Pallas kernels for 0%

profile of v1, /device:TPU:1, one launch (start us, length us, event | category | flops | bytes accessed | tf_op | source)
XLA Modules:
  0.0 974.6 jit_solution(10541210328815648130)
XLA Ops:
  27.0 10.5 %psum.169 = f32[32]{0:T(128)S(1)} all-reduce(f32[32]{0:T(128)S(1)} %get-tuple-element.44), channel_id=1, replica_groups=mesh['sx'=8,'sy'=4] {'sy'}, use_global_device_ids=true, to_apply=%region_15.19 | all-reduce | flops 32 | bytes 256 | tf_op jit(solution)/shard_map/psum | solution.py:89
  37.5 14.5 %psum.170 = f32[32]{0:T(128)S(1)} all-reduce(f32[32]{0:T(128)S(1)} %psum.169), channel_id=1, replica_groups=mesh['sx'=8,'sy'=4] {'sx'}, use_global_device_ids=true, to_apply=%region_16.20 | all-reduce | flops 32 | bytes 256 | tf_op jit(solution)/shard_map/psum | solution.py:89
  52.0 37.5 %psum.168 = f32[32]{0:T(128)S(1)} all-reduce(f32[32]{0:T(128)S(1)} %get-tuple-element.45), channel_id=1, replica_groups=mesh['sx'=8,'sy'=4] {'sx','sy'}, use_global_device_ids=true, to_apply=%region_9.13 | all-reduce | flops 32 | bytes 256 | tf_op jit(solution)/shard_map/psum | solution.py:78
  90.8 44.0 %psum.171 = f32[32]{0:T(128)S(1)} all-reduce(f32[32]{0:T(128)S(1)} %multiply_reduce_fusion.12), channel_id=1, replica_groups=mesh['sx'=8,'sy'=4] {'sx','sy'}, use_global_device_ids=true, to_apply=%region_18.22 | all-reduce | flops 32 | bytes 256 | tf_op jit(solution)/shard_map/psum | solution.py:78
  153.3 10.0 %psum.172 = f32[32]{0:T(128)S(1)} all-reduce(f32[32]{0:T(128)S(1)} %get-tuple-element.107), channel_id=1, replica_groups=mesh['sx'=8,'sy'=4] {'sy'}, use_global_device_ids=true, to_apply=%region_20.24 | all-reduce | flops 32 | bytes 256 | tf_op jit(solution)/shard_map/psum | solution.py:89
  163.3 13.8 %psum.173 = f32[32]{0:T(128)S(1)} all-reduce(f32[32]{0:T(128)S(1)} %psum.172), channel_id=1, replica_groups=mesh['sx'=8,'sy'=4] {'sx'}, use_global_device_ids=true, to_apply=%region_21.25 | all-reduce | flops 32 | bytes 256 | tf_op jit(solution)/shard_map/psum | solution.py:89
  177.2 37.7 %psum.174 = f32[32]{0:T(128)S(1)} all-reduce(f32[32]{0:T(128)S(1)} %get-tuple-element.72), channel_id=1, replica_groups=mesh['sx'=8,'sy'=4] {'sx','sy'}, use_global_device_ids=true, to_apply=%region_23.27 | all-reduce | flops 32 | bytes 256 | tf_op jit(solution)/shard_map/psum | solution.py:78
  245.5 15.4 %psum.176 = f32[32]{0:T(128)S(1)} all-reduce(f32[32]{0:T(128)S(1)} %psum.175), channel_id=1, replica_groups=mesh['sx'=8,'sy'=4] {'sx'}, use_global_device_ids=true, to_apply=%region_26.30 | all-reduce | flops 32 | bytes 256 | tf_op jit(solution)/shard_map/psum | solution.py:89
  260.9 37.1 %psum.177 = f32[32]{0:T(128)S(1)} all-reduce(f32[32]{0:T(128)S(1)} %get-tuple-element.70), channel_id=1, replica_groups=mesh['sx'=8,'sy'=4] {'sx','sy'}, use_global_device_ids=true, to_apply=%region_28.32 | all-reduce | flops 32 | bytes 256 | tf_op jit(solution)/shard_map/psum | solution.py:78
  325.3 14.3 %psum.179 = f32[32]{0:T(128)S(1)} all-reduce(f32[32]{0:T(128)S(1)} %psum.178), channel_id=1, replica_groups=mesh['sx'=8,'sy'=4] {'sx'}, use_global_device_ids=true, to_apply=%region_31.35 | all-reduce | flops 32 | bytes 256 | tf_op jit(solution)/shard_map/psum | solution.py:89
  339.6 36.5 %psum.180 = f32[32]{0:T(128)S(1)} all-reduce(f32[32]{0:T(128)S(1)} %get-tuple-element.68), channel_id=1, replica_groups=mesh['sx'=8,'sy'=4] {'sx','sy'}, use_global_device_ids=true, to_apply=%region_33.37 | all-reduce | flops 32 | bytes 256 | tf_op jit(solution)/shard_map/psum | solution.py:78
  402.1 14.9 %psum.182 = f32[32]{0:T(128)S(1)} all-reduce(f32[32]{0:T(128)S(1)} %psum.181), channel_id=1, replica_groups=mesh['sx'=8,'sy'=4] {'sx'}, use_global_device_ids=true, to_apply=%region_36.40 | all-reduce | flops 32 | bytes 256 | tf_op jit(solution)/shard_map/psum | solution.py:89
  417.1 37.1 %psum.183 = f32[32]{0:T(128)S(1)} all-reduce(f32[32]{0:T(128)S(1)} %get-tuple-element.66), channel_id=1, replica_groups=mesh['sx'=8,'sy'=4] {'sx','sy'}, use_global_device_ids=true, to_apply=%region_38.42 | all-reduce | flops 32 | bytes 256 | tf_op jit(solution)/shard_map/psum | solution.py:78
  481.3 14.5 %psum.185 = f32[32]{0:T(128)S(1)} all-reduce(f32[32]{0:T(128)S(1)} %psum.184), channel_id=1, replica_groups=mesh['sx'=8,'sy'=4] {'sx'}, use_global_device_ids=true, to_apply=%region_41.45 | all-reduce | flops 32 | bytes 256 | tf_op jit(solution)/shard_map/psum | solution.py:89
  495.8 37.1 %psum.186 = f32[32]{0:T(128)S(1)} all-reduce(f32[32]{0:T(128)S(1)} %get-tuple-element.64), channel_id=1, replica_groups=mesh['sx'=8,'sy'=4] {'sx','sy'}, use_global_device_ids=true, to_apply=%region_43.47 | all-reduce | flops 32 | bytes 256 | tf_op jit(solution)/shard_map/psum | solution.py:78
  558.3 16.1 %psum.188 = f32[32]{0:T(128)S(1)} all-reduce(f32[32]{0:T(128)S(1)} %psum.187), channel_id=1, replica_groups=mesh['sx'=8,'sy'=4] {'sx'}, use_global_device_ids=true, to_apply=%region_46.50 | all-reduce | flops 32 | bytes 256 | tf_op jit(solution)/shard_map/psum | solution.py:89
  574.4 37.1 %psum.189 = f32[32]{0:T(128)S(1)} all-reduce(f32[32]{0:T(128)S(1)} %multiply_reduce_fusion), channel_id=1, replica_groups=mesh['sx'=8,'sy'=4] {'sx','sy'}, use_global_device_ids=true, to_apply=%region_48.52 | all-reduce | flops 32 | bytes 256 | tf_op jit(solution)/shard_map/psum | solution.py:78
  626.5 23.9 %collective-permute-done.36 = f32[3,1,6,32]{3,2,1,0:T(8,128)S(1)} collective-permute-done((f32[3,1,6,32]{3,2,1,0:T(8,128)S(1)}, f32[3,1,6,32]{3,2,1,0:T(8,128)S(1)}, u32[]{:S(2)}, u32[]{:S(2)}) %collective-permute-start.36) | collective-permute-done | bytes 2336 | tf_op jit(solution)/shard_map/ppermute | solution.py:26
  664.3 14.6 %psum.191 = f32[32]{0:T(128)S(1)} all-reduce(f32[32]{0:T(128)S(1)} %psum.190), channel_id=1, replica_groups=mesh['sx'=8,'sy'=4] {'sx'}, use_global_device_ids=true, to_apply=%region_51.55 | all-reduce | flops 32 | bytes 256 | tf_op jit(solution)/shard_map/psum | solution.py:89
  682.7 11.7 %cholesky.286 = f32[128,128]{1,0:T(8,128)S(1)} custom-call(f32[128,128]{1,0:T(8,128)S(1)} %cholesky.426), custom_call_target="Cholesky" | custom-call | tf_op jit(solution)/shard_map/jit(cholesky)/cholesky | solution.py:35
  706.9 11.7 %cholesky.305 = f32[128,128]{1,0:T(8,128)S(1)} custom-call(f32[128,128]{1,0:T(8,128)S(1)} %cholesky.430), custom_call_target="Cholesky" | custom-call | tf_op jit(solution)/shard_map/jit(cholesky)/cholesky | solution.py:35
  718.6 10.2 %custom-call.32 = f32[1,128,128]{1,2,0:T(8,128)S(1)} custom-call(f32[1,128,128]{2,1,0:T(8,128)S(1)} %get-tuple-element.100), custom_call_target="InvertDiagBlocksLowerTriangular" | custom-call | tf_op jit(solution)/shard_map/jit(cholesky)/cholesky | solution.py:35
  730.4 11.7 %cholesky.326 = f32[128,128]{1,0:T(8,128)S(1)} custom-call(f32[128,128]{1,0:T(8,128)S(1)} %cholesky.435), custom_call_target="Cholesky" | custom-call | tf_op jit(solution)/shard_map/jit(cholesky)/cholesky | solution.py:35
  754.1 11.9 %cholesky.343 = f32[128,128]{1,0:T(8,128)S(1)} custom-call(f32[128,128]{1,0:T(8,128)S(1)} %slice_subtract_fusion.5), custom_call_target="Cholesky" | custom-call | tf_op jit(solution)/shard_map/jit(cholesky)/cholesky | solution.py:35
  770.7 10.3 %while.8 = (s32[]{:T(128)}, f32[512,512]{1,0:T(8,128)S(1)}, s32[4,2]{0,1:T(2,128)S(1)}, f32[4,128,128]{2,1,0:T(8,128)}, s32[]{:T(128)}) while((s32[]{:T(128)}, f32[512,512]{1,0:T(8,128)S(1)}, s32[4,2]{0,1:T(2,128)S(1)}, f32[4,128,128]{2,1,0:T(8,128)}, s32[]{:T(128)}) %tuple.84), condition=%wide.while_cond.1, body=%wide.while_body.1.sunk | while | flops 2 | bytes 132205 | solution.py:38
  781.0 40.7 %custom-call.35 = f32[4,128,128]{1,2,0:T(8,128)} custom-call(f32[4,128,128]{2,1,0:T(8,128)} %get-tuple-element.35), custom_call_target="InvertDiagBlocksLowerTriangular" | custom-call | tf_op jit(solution)/shard_map/jit(_solve_triangular)/triangular_solve | solution.py:38
  833.6 11.7 %cholesky.358 = f32[128,128]{1,0:T(8,128)S(1)} custom-call(f32[128,128]{1,0:T(8,128)S(1)} %cholesky.439), custom_call_target="Cholesky" | custom-call | tf_op jit(solution)/shard_map/jit(cholesky)/cholesky | solution.py:35
  855.9 11.7 %cholesky.377 = f32[128,128]{1,0:T(8,128)S(1)} custom-call(f32[128,128]{1,0:T(8,128)S(1)} %cholesky.443), custom_call_target="Cholesky" | custom-call | tf_op jit(solution)/shard_map/jit(cholesky)/cholesky | solution.py:35
  867.7 10.0 %custom-call.37 = f32[1,128,128]{1,2,0:T(8,128)S(1)} custom-call(f32[1,128,128]{2,1,0:T(8,128)S(1)} %get-tuple-element.90), custom_call_target="InvertDiagBlocksLowerTriangular" | custom-call | tf_op jit(solution)/shard_map/jit(cholesky)/cholesky | solution.py:35
  878.4 11.7 %cholesky.398 = f32[128,128]{1,0:T(8,128)S(1)} custom-call(f32[128,128]{1,0:T(8,128)S(1)} %cholesky.448), custom_call_target="Cholesky" | custom-call | tf_op jit(solution)/shard_map/jit(cholesky)/cholesky | solution.py:35
  901.2 11.7 %cholesky.415 = f32[128,128]{1,0:T(8,128)S(1)} custom-call(f32[128,128]{1,0:T(8,128)S(1)} %slice_subtract_fusion.4), custom_call_target="Cholesky" | custom-call | tf_op jit(solution)/shard_map/jit(cholesky)/cholesky | solution.py:35
  925.5 39.3 %custom-call.40 = f32[4,128,128]{1,2,0:T(8,128)S(1)} custom-call(f32[4,128,128]{2,1,0:T(8,128)S(1)} %get-tuple-element.37), custom_call_target="InvertDiagBlocksLowerTriangular" | custom-call | tf_op jit(solution)/shard_map/jit(_solve_triangular)/triangular_solve | solution.py:38
  (328 shorter events, 314.8 us)
Async XLA Ops:
  3.7 14.8 %collective-permute-start.6 = (f32[1,1,6,32]{3,2,1,0:T(8,128)S(1)}, f32[1,1,6,32]{3,2,1,0:T(8,128)S(1)}, u32[]{:S(2)}, u32[]{:S(2)}) collective-permute-start(f32[1,1,6,32]{3,2,1,0:T(8,128)S(1)} %bitcast.395), channel_id=1, source_target_pairs={{4,0},{8,4},{12,8},{16,12},{20,16},{24,20},{28,24},{5,1},{9,5},{13... | collective-permute-start | bytes 2312 | tf_op jit(solution)/shard_map/ppermute | solution.py:26
  5.6 12.9 %collective-permute-start.5 = (f32[1,1,6,32]{3,2,1,0:T(8,128)S(1)}, f32[1,1,6,32]{3,2,1,0:T(8,128)S(1)}, u32[]{:S(2)}, u32[]{:S(2)}) collective-permute-start(f32[1,1,6,32]{3,2,1,0:T(8,128)S(1)} %bitcast.396), channel_id=1, source_target_pairs={{0,4},{4,8},{8,12},{12,16},{16,20},{20,24},{24,28},{1,5},{5,9},{9,... | collective-permute-start | bytes 2312 | tf_op jit(solution)/shard_map/ppermute | solution.py:24
  10.8 6.1 collective-permute-start.4
  18.5 6.1 collective-permute-start.8
  89.5 875.3 %collective-permute-start.38 = (f32[32,512]{1,0:T(8,128)}, f32[32,512]{1,0:T(8,128)}, u32[]{:S(2)}, u32[]{:S(2)}) collective-permute-start(f32[32,512]{1,0:T(8,128)} %slice_bitcast_fusion.8), channel_id=1, source_target_pairs={{1,0},{2,1},{3,2},{5,4},{6,5},{7,6},{9,8},{10,9},{11,10},{13,12},{... | collective-permute-start | bytes 196616 | tf_op jit(solution)/shard_map/ppermute | solution.py:13
  134.8 10.6 %collective-permute-start.10 = (f32[1,1,6,32]{3,2,1,0:T(8,128)S(1)}, f32[1,1,6,32]{3,2,1,0:T(8,128)S(1)}, u32[]{:S(2)}, u32[]{:S(2)}) collective-permute-start(f32[1,1,6,32]{3,2,1,0:T(8,128)S(1)} %bitcast.414), channel_id=1, source_target_pairs={{4,0},{8,4},{12,8},{16,12},{20,16},{24,20},{28,24},{5,1},{9,5},{13... | collective-permute-start | bytes 2312 | tf_op jit(solution)/shard_map/ppermute | solution.py:26
  138.2 7.2 collective-permute-start.9
  143.5 678.3 %collective-permute-start.1 = (f32[32,512]{1,0:T(8,128)}, f32[32,512]{1,0:T(8,128)}, u32[]{:S(2)}, u32[]{:S(2)}) collective-permute-start(f32[32,512]{1,0:T(8,128)} %slice_bitcast_fusion.9), channel_id=1, source_target_pairs={{4,0},{8,4},{12,8},{16,12},{20,16},{24,20},{28,24},{5,1},{9,5},{13... | collective-permute-start | bytes 196616 | tf_op jit(solution)/shard_map/ppermute | solution.py:13
  214.9 13.1 %collective-permute-start.14 = (f32[1,1,6,32]{3,2,1,0:T(8,128)S(1)}, f32[1,1,6,32]{3,2,1,0:T(8,128)S(1)}, u32[]{:S(2)}, u32[]{:S(2)}) collective-permute-start(f32[1,1,6,32]{3,2,1,0:T(8,128)S(1)} %bitcast.399), channel_id=1, source_target_pairs={{4,0},{8,4},{12,8},{16,12},{20,16},{24,20},{28,24},{5,1},{9,5},{13... | collective-permute-start | bytes 2312 | tf_op jit(solution)/shard_map/ppermute | solution.py:26
  218.2 9.8 %collective-permute-start.13 = (f32[1,1,6,32]{3,2,1,0:T(8,128)S(1)}, f32[1,1,6,32]{3,2,1,0:T(8,128)S(1)}, u32[]{:S(2)}, u32[]{:S(2)}) collective-permute-start(f32[1,1,6,32]{3,2,1,0:T(8,128)S(1)} %bitcast.400), channel_id=1, source_target_pairs={{0,4},{4,8},{8,12},{12,16},{16,20},{20,24},{24,28},{1,5},{5,9},{9,... | collective-permute-start | bytes 2312 | tf_op jit(solution)/shard_map/ppermute | solution.py:24
  226.0 454.9 %collective-permute-start = (f32[512,512]{0,1:T(8,128)}, f32[512,512]{0,1:T(8,128)S(1)}, u32[]{:S(2)}, u32[]{:S(2)}) collective-permute-start(f32[512,512]{0,1:T(8,128)} %bitcast.3), channel_id=1, source_target_pairs={{4,0},{8,4},{12,8},{16,12},{20,16},{24,20},{28,24},{5,1},{9,5},{13... | collective-permute-start | bytes 3145736 | tf_op jit(solution)/shard_map/ppermute | solution.py:13
  228.0 6.6 collective-permute-start.16
  229.3 5.9 collective-permute-start.15
  298.0 10.4 %collective-permute-start.18 = (f32[1,1,6,32]{3,2,1,0:T(8,128)S(1)}, f32[1,1,6,32]{3,2,1,0:T(8,128)S(1)}, u32[]{:S(2)}, u32[]{:S(2)}) collective-permute-start(f32[1,1,6,32]{3,2,1,0:T(8,128)S(1)} %bitcast.402), channel_id=1, source_target_pairs={{4,0},{8,4},{12,8},{16,12},{20,16},{24,20},{28,24},{5,1},{9,5},{13... | collective-permute-start | bytes 2312 | tf_op jit(solution)/shard_map/ppermute | solution.py:26
  301.5 6.9 collective-permute-start.17
  308.4 6.1 collective-permute-start.20
  309.7 5.5 collective-permute-start.19
  376.2 8.9 collective-permute-start.22
  379.5 5.5 collective-permute-start.21
  385.1 6.2 collective-permute-start.24
  386.5 5.5 collective-permute-start.23
  454.2 9.5 collective-permute-start.26
  457.6 6.1 collective-permute-start.25
  463.7 6.1 collective-permute-start.28
  532.9 7.9 collective-permute-start.30
  540.8 6.1 collective-permute-start.32
  542.1 5.5 collective-permute-start.31
  611.5 11.6 %collective-permute-start.34 = (f32[1,1,6,32]{3,2,1,0:T(8,128)S(1)}, f32[1,1,6,32]{3,2,1,0:T(8,128)S(1)}, u32[]{:S(2)}, u32[]{:S(2)}) collective-permute-start(f32[1,1,6,32]{3,2,1,0:T(8,128)S(1)} %bitcast.417), channel_id=1, source_target_pairs={{4,0},{8,4},{12,8},{16,12},{20,16},{24,20},{28,24},{5,1},{9,5},{13... | collective-permute-start | bytes 2312 | tf_op jit(solution)/shard_map/ppermute | solution.py:26
  614.9 9.5 collective-permute-start.33
  623.1 208.4 %collective-permute-start.37 = (f32[512,512]{0,1:T(8,128)}, f32[512,512]{0,1:T(8,128)}, u32[]{:S(2)}, u32[]{:S(2)}) collective-permute-start(f32[512,512]{0,1:T(8,128)} %bitcast.390), channel_id=1, source_target_pairs={{1,0},{2,1},{3,2},{5,4},{6,5},{7,6},{9,8},{10,9},{11,10},{13,12},{... | collective-permute-start | bytes 3145736 | tf_op jit(solution)/shard_map/ppermute | solution.py:13
  625.1 25.3 %collective-permute-start.36 = (f32[3,1,6,32]{3,2,1,0:T(8,128)S(1)}, f32[3,1,6,32]{3,2,1,0:T(8,128)S(1)}, u32[]{:S(2)}, u32[]{:S(2)}) collective-permute-start(f32[3,1,6,32]{3,2,1,0:T(8,128)S(1)} %pad_maximum_fusion.7), channel_id=1, source_target_pairs={{1,0},{2,1},{3,2},{5,4},{6,5},{7,6},{9,8},{10,9},{11,10},{13,12},{... | collective-permute-start | bytes 6920 | tf_op jit(solution)/shard_map/ppermute | solution.py:26
  829.6 141.7 %collective-permute-start.2 = (f32[32,512]{1,0:T(8,128)}, f32[32,512]{1,0:T(8,128)}, u32[]{:S(2)}, u32[]{:S(2)}) collective-permute-start(f32[32,512]{1,0:T(8,128)} %get-tuple-element.75), channel_id=1, source_target_pairs={{0,4},{4,8},{8,12},{12,16},{16,20},{20,24},{24,28},{1,5},{5,9},{9,... | collective-permute-start | bytes 196616 | tf_op jit(solution)/shard_map/ppermute | solution.py:13
  (29 other events, 1495.4 us)
